TPU v7x, 32 devices: a whole 2x2x4 slice. The times are simulated.
32 devices in a mesh: scene: 2 (over y), rows: 4 (over z), cols: 2 (over x), chan: 2 (over core).
Axes of the slice: x: 2, y: 2, z: 4, core: 2. Of those that a mesh axis runs over, the one named last changes fastest.
Arguments:
- position: float32 [3, 4096], P(None, ('scene', 'rows', 'cols', 'chan')), parts along dimension 1, may hold values from 0 to 1
- tilt: float32 [2, 4096], P(None, ('scene', 'rows', 'cols', 'chan')), parts along dimension 1, may hold values from -3.140625 to 3.140625
- patch_area: float32 [4096], P(('scene', 'rows', 'cols', 'chan')), parts along dimension 0, may hold values from 0.005859375 to 0.0234375
- reflect: float32 [3, 4096], P(None, ('scene', 'rows', 'cols', 'chan')), parts along dimension 1, may hold values from 0.2 to 0.9
- emission: float32 [96, 4096], P(None, ('scene', 'rows', 'cols', 'chan')), parts along dimension 1, may hold values from 0.05 to 1
- radiosity: bfloat16 [96, 4096], P(None, ('scene', 'rows', 'cols', 'chan')), parts along dimension 1, may hold values from 0.25 to 2
- cotangent: bfloat16 [96, 4096], P(None, ('scene', 'rows', 'cols', 'chan')), parts along dimension 1, may hold values from -0.5 to 1.5
- block_inverse: bfloat16 [8, 512, 512], P(('scene', 'rows')), parts along dimension 0, may hold values from -1 to 2
- visibility: int32 [32, 16], P('scene'), parts along dimension 0, may hold values from 0 to 1
- cluster_ids: int32 [8], P('scene'), parts along dimension 0, may hold values from 0 to 3, each once
Outputs:
- radiosity_next: bfloat16 [96, 4096], P(None, ('scene', 'rows', 'cols', 'chan')), parts along dimension 1
- gradient: float32 [96, 4096], P(None, ('scene', 'rows', 'cols', 'chan')), parts along dimension 1
There are 2 independent parts, one for each index of `scene`. A program takes and returns all parts, laid end to end along the dimension named above; each array names one. Nothing has to cross between parts.
All inputs are finite; a program needn't handle non-finite values.
Results may differ from a plain program's by a relative error of at most 0.0095.
Values may be sent and summed in bfloat16 or wider, within the bound.
No kernel may reach another device: no remote copies, remote signals or barrier semaphores. Data moves between devices by JAX's collectives and lax.ppermute only.
A program may use at most 64 MiB of HBM per device.

v0:
```python
import math

import jax
import jax.numpy as jnp
from jax import lax
from jax.sharding import PartitionSpec as P

CLUSTER = 512
SUB = 128


def normals(tilt):
    a = tilt[0]
    b = tilt[1]
    return jnp.stack([jnp.cos(a) * jnp.cos(b), jnp.sin(a) * jnp.cos(b), jnp.sin(b)])


def factors(recv_pos, recv_normal, src_pos, src_normal, src_area, visible):
    offset_vec = src_pos[:, None, :] - recv_pos[:, :, None]
    distance = jnp.sum(offset_vec * offset_vec, axis=0)
    facing = jnp.sum(recv_normal[:, :, None] * offset_vec, axis=0)
    behind = -jnp.sum(src_normal[:, None, :] * offset_vec, axis=0)
    spread = distance + src_area[None, :]
    value = (
        jnp.maximum(facing, 0.0)
        * jnp.maximum(behind, 0.0)
        * src_area[None, :]
        / (jnp.pi * spread * spread)
    )
    return (value * visible).astype(jnp.bfloat16)


def split_parts(values):
    upper = values.astype(jnp.bfloat16)
    lower = (values - upper.astype(jnp.float32)).astype(jnp.bfloat16)
    return (upper, lower)


def local(
    position,
    tilt,
    patch_area,
    reflect,
    emission,
    radiosity,
    cotangent,
    block_inverse,
    visibility,
    cluster_ids,
):
    dev_patches = position.shape[1]
    channels = radiosity.shape[0]
    lights = channels // 3
    row_patches = dev_patches * lax.axis_size(("cols", "chan"))
    column_index = lax.axis_index(("cols", "chan"))
    row_index = lax.axis_index("rows")
    sub_count = CLUSTER // SUB
    own_offset = column_index * dev_patches
    own_cluster = own_offset // CLUSTER
    own_inverse = lax.dynamic_index_in_dim(block_inverse, own_cluster, 0, keepdims=False)
    rho_own = jnp.tile(reflect, (lights, 1))
    own_geom = jnp.concatenate([position, tilt, patch_area[None, :]], axis=0)
    recv_all = lax.all_gather(
        jnp.concatenate([own_geom, reflect], axis=0), ("cols", "chan"), axis=1, tiled=True
    )
    recv_cot = lax.all_gather(cotangent, ("cols", "chan"), axis=1, tiled=True)
    src_geom = lax.all_gather(own_geom, "rows", axis=1, tiled=True)
    recv_pos = recv_all[0:3]
    recv_normal = normals(recv_all[3:5])
    sub_start = row_index * row_patches + jnp.arange(row_patches // SUB, dtype=jnp.int32) * SUB
    recv_cluster = sub_start // CLUSTER
    recv_block = jnp.take(cluster_ids, recv_cluster) * sub_count + sub_start % CLUSTER // SUB
    visible_rows = jnp.take(visibility, recv_block, axis=0)
    cot_cluster = lax.dynamic_slice_in_dim(recv_cot, own_cluster * CLUSTER, CLUSTER, 1)
    inverse_columns = lax.dynamic_slice_in_dim(own_inverse, own_offset % CLUSTER, dev_patches, 1)
    adjoint_own = jnp.dot(cot_cluster, inverse_columns, preferred_element_type=jnp.float32)
    weight_own = (rho_own * adjoint_own).astype(jnp.bfloat16)
    weight = lax.all_gather(weight_own, ("cols", "chan"), axis=1, tiled=True)
    initial = (
        jnp.zeros((channels, row_patches), jnp.float32),
        jnp.zeros((channels, src_geom.shape[1]), jnp.float32),
    )
    piece = lax.all_gather(radiosity, "rows", axis=1, tiled=True)
    piece_len = piece.shape[1]
    step_width = math.gcd(piece_len, 256)

    def column_block(totals, j):
        offset = j * step_width
        piece_rad = lax.dynamic_slice_in_dim(piece, j * step_width, step_width, 1)
        piece_geom = lax.dynamic_slice_in_dim(src_geom, offset, step_width, 1)
        q = offset + jnp.arange(step_width, dtype=jnp.int32)
        p = q // dev_patches * row_patches + column_index * dev_patches + q % dev_patches
        src_cluster = p // CLUSTER
        src_block = jnp.take(cluster_ids, src_cluster) * sub_count + p % CLUSTER // SUB
        visible_sub = jnp.take(visible_rows, src_block, axis=1).astype(jnp.float32)
        visible_sub = visible_sub * (recv_cluster[:, None] != src_cluster[None, :]).astype(
            jnp.float32
        )
        visible = jnp.repeat(visible_sub, SUB, axis=0)
        factor_tile = factors(
            recv_pos, recv_normal, piece_geom[0:3], normals(piece_geom[3:5]), piece_geom[5], visible
        )
        gathered = lax.dot_general(
            piece_rad, factor_tile, (((1,), (1,)), ((), ())), preferred_element_type=jnp.float32
        )
        column = jnp.dot(weight, factor_tile, preferred_element_type=jnp.float32)
        gathered, column = (gathered, column)
        forward, adjoint = totals
        adjoint = lax.dynamic_update_slice_in_dim(adjoint, column, offset, 1)
        return ((forward + gathered, adjoint), None)

    result, unused = lax.scan(
        column_block, initial, jnp.arange(piece_len // step_width, dtype=jnp.int32)
    )
    forward, adjoint = result
    gradient = lax.psum_scatter(
        adjoint.astype(jnp.bfloat16), "rows", scatter_dimension=1, tiled=True
    ).astype(jnp.float32)
    summed = lax.psum_scatter(
        forward.astype(jnp.bfloat16), ("cols", "chan"), scatter_dimension=1, tiled=True
    ).astype(jnp.float32)
    terms = emission + rho_own * summed
    row_terms = lax.all_gather(
        terms.astype(jnp.bfloat16), ("cols", "chan"), axis=1, tiled=True
    ).astype(terms.dtype)
    vector = lax.dynamic_slice_in_dim(row_terms, own_cluster * CLUSTER, CLUSTER, 1)
    inverse_rows = lax.dynamic_slice_in_dim(own_inverse, own_offset % CLUSTER, dev_patches, 0)
    upper, lower = split_parts(vector)
    dims = (((1,), (1,)), ((), ()))
    solved = lax.dot_general(upper, inverse_rows, dims, preferred_element_type=jnp.float32)
    solved = solved + lax.dot_general(lower, inverse_rows, dims, preferred_element_type=jnp.float32)
    result = solved.astype(jnp.bfloat16)
    return (result, gradient)


def solution(mesh):
    return jax.shard_map(
        local,
        mesh=mesh,
        in_specs=(
            P(None, ("scene", "rows", "cols", "chan")),
            P(None, ("scene", "rows", "cols", "chan")),
            P(("scene", "rows", "cols", "chan")),
            P(None, ("scene", "rows", "cols", "chan")),
            P(None, ("scene", "rows", "cols", "chan")),
            P(None, ("scene", "rows", "cols", "chan")),
            P(None, ("scene", "rows", "cols", "chan")),
            P(("scene", "rows"), None, None),
            P("scene", None),
            P("scene"),
        ),
        out_specs=(
            P(None, ("scene", "rows", "cols", "chan")),
            P(None, ("scene", "rows", "cols", "chan")),
        ),
        check_vma=False,
    )
```

profile of v0, /device:TPU:0, one launch (start us, length us, event | category | flops | bytes accessed | tf_op | source)
XLA Modules:
  0.0 116.8 jit_solution(3368443143671929076)
XLA Ops:
  7.2 0.0 reduce-scatter.7.cloned.1.call-start
  7.3 1.3 %gather_fusion.1 = s32[4]{0:T(128)S(1)} fusion(s32[4]{0:T(128)} %param.21, s32[1024]{0:T(1024)S(1)} %pad_clamp_fusion.2), kind=kCustom, calls=%fused_computation.1 | custom fusion | bytes 48 | tf_op jit(solution)/shard_map/jit(_take)/gather | solution.py:72
  8.7 6.2 %all_gather.19 = f32[9,512]{1,0:T(8,128)S(1)} all-gather(f32[9,128]{1,0:T(8,128)S(1)} %pad_maximum_fusion.1), channel_id=1, replica_groups=mesh['scene'=2,'rows'=4,'cols'=2,'chan'=2] {'cols','chan'}, dimensions={1}, use_global_device_ids=true | all-gather | bytes 23040 | tf_op jit(solution)/shard_map/all_gather | solution.py:63
  15.0 0.1 cosine_multiply_fusion.1
  15.2 5.6 %all_gather.21 = bf16[96,512]{1,0:T(8,128)(2,1)S(1)} all-gather(bf16[96,128]{1,0:T(8,128)(2,1)S(1)} %copy-done.4), channel_id=1, replica_groups=mesh['scene'=2,'rows'=4,'cols'=2,'chan'=2] {'cols','chan'}, dimensions={1}, use_global_device_ids=true | all-gather | bytes 122880 | tf_op jit(solution)/shard_map/all_gather | solution.py:66
  20.8 0.2 fusion.17
  21.0 5.4 %all_gather.22 = bf16[96,512]{1,0:T(8,128)(2,1)S(1)} all-gather(bf16[96,128]{1,0:T(8,128)(2,1)S(1)} %fusion.17), channel_id=1, replica_groups=mesh['scene'=2,'rows'=4,'cols'=2,'chan'=2] {'cols','chan'}, dimensions={1}, use_global_device_ids=true | all-gather | bytes 122880 | tf_op jit(solution)/shard_map/all_gather | solution.py:78
  26.3 0.6 gather_fusion.2
  26.9 0.1 broadcast_select_fusion
  27.0 0.1 copy.19
  27.1 13.6 %all_gather.20 = f32[6,512]{1,0:T(8,128)S(1)} all-gather(f32[6,128]{1,0:T(8,128)S(1)} %pad_maximum_fusion.3), channel_id=1, replica_groups=mesh['scene'=2,'rows'=4,'cols'=2,'chan'=2] {'rows'}, dimensions={1}, use_global_device_ids=true | all-gather | bytes 15360 | tf_op jit(solution)/shard_map/all_gather | solution.py:67
  40.7 12.1 %all_gather.18 = bf16[96,512]{1,0:T(8,128)(2,1)S(1)} all-gather(bf16[96,128]{1,0:T(8,128)(2,1)S(1)} %copy-done.5), channel_id=1, replica_groups=mesh['scene'=2,'rows'=4,'cols'=2,'chan'=2] {'rows'}, dimensions={1}, use_global_device_ids=true | all-gather | bytes 122880 | tf_op jit(solution)/shard_map/all_gather | solution.py:83
  52.9 13.5 %while.16 = (s32[]{:T(128)}, f32[96,512]{1,0:T(8,128)S(1)}, bf16[96,512]{1,0:T(8,128)(2,1)S(1)}, s32[2]{0:T(128)S(1)}, bf16[96,512]{1,0:T(8,128)(2,1)S(1)}, /*in...) while((s32[]{:T(128)}, f32[96,512]{1,0:T(8,128)S(1)}, ...), condition=%wide.region_4.5_spmd.clone, body=%wide.region_0.4_spmd.clone.sunk | while | flops 54285644 | bytes 4650917 | solution.py:112
  52.9 0.6 dynamic_slice.60
  54.1 0.2 fusion.50
  54.2 0.5 fusion.51
  54.7 0.7 fusion.52
  55.4 2.5 %compare_select_fusion.37 = (s32[256,1]{0,1:T(1,128)S(1)}, s32[256,1]{0,1:T(1,128)S(1)}) fusion(s32[]{:T(128)} %get-tuple-element.519, s32[]{:T(128)} %bitcast.70, s32[]{:T(128)} %bitcast.71, s32[]{:T(128)} %bitcast.72, s32[]{:T(128)} %bitcast.73, s32[]{:T(128)} %bitcast.74), kind=kLoop, calls=%fused_computation.19.clone.1 | loop fusion | flops 19200 | bytes 2072 | tf_op jit(solution)/shard_map/while/body/eval_jaxpr/jit(_take)/jit(_where)/select_n | solution.py:95
  58.0 0.7 gather_fusion
  58.7 0.1 bitcast_select_fusion.2
  58.9 0.1 copy.25
  59.0 0.2 fusion.53
  59.2 0.2 convolution_add_fusion.3
  59.4 0.2 fusion.54
  59.6 0.6 dynamic_slice.60
  60.8 0.2 fusion.50
  61.0 0.5 fusion.51
  61.5 0.7 fusion.52
  62.1 2.5 %compare_select_fusion.37 = (s32[256,1]{0,1:T(1,128)S(1)}, s32[256,1]{0,1:T(1,128)S(1)}) fusion(s32[]{:T(128)} %get-tuple-element.519, s32[]{:T(128)} %bitcast.70, s32[]{:T(128)} %bitcast.71, s32[]{:T(128)} %bitcast.72, s32[]{:T(128)} %bitcast.73, s32[]{:T(128)} %bitcast.74), kind=kLoop, calls=%fused_computation.19.clone.1 | loop fusion | flops 19200 | bytes 2072 | tf_op jit(solution)/shard_map/while/body/eval_jaxpr/jit(_take)/jit(_where)/select_n | solution.py:95
  64.7 0.7 gather_fusion
  65.5 0.1 bitcast_select_fusion.2
  65.6 0.1 copy.25
  65.7 0.2 fusion.53
  65.9 0.2 convolution_add_fusion.3
  66.2 0.2 fusion.54
  66.4 0.8 copy.20
  67.2 0.0 reduce-scatter.7.cloned.1.call-update
  67.2 0.0 reduce-scatter.9.cloned.1.call-start
  67.2 0.8 copy.22
  68.0 0.0 reduce-scatter.9.cloned.1.call-update
  68.0 18.8 %reduce-scatter.7.cloned.1.call-done = bf16[128,96]{1,0:T(8,128)(2,1)} async-done(((bf16[512,96]{1,0:T(8,128)(2,1)}), bf16[128,96]{1,0:T(8,128)(2,1)}) %reduce-scatter.7.cloned.1.call-update) | async-done | bytes 24592
  86.8 0.8 copy.21
  87.7 5.4 %all_gather.23 = bf16[96,512]{1,0:T(8,128)(2,1)S(1)} all-gather(bf16[96,128]{1,0:T(8,128)(2,1)S(1)} %add_convert_fusion), channel_id=1, replica_groups=mesh['scene'=2,'rows'=4,'cols'=2,'chan'=2] {'cols','chan'}, dimensions={1}, use_global_device_ids=true | all-gather | bytes 122880 | tf_op jit(solution)/shard_map/all_gather | solution.py:123
  93.0 0.2 fusion.19
  93.2 0.8 fusion.16
  94.0 14.5 %reduce-scatter.9.cloned.1.call-done = bf16[128,96]{1,0:T(8,128)(2,1)} async-done(((bf16[512,96]{1,0:T(8,128)(2,1)}), bf16[128,96]{1,0:T(8,128)(2,1)}) %reduce-scatter.9.cloned.1.call-update) | async-done | bytes 24592
  108.5 0.8 copy.23
  109.3 0.6 convert_element_type.52
  (46 shorter events, 0.4 us)
Async XLA Ops:
  7.2 13.6 %copy-start = (bf16[1,512,512]{2,1,0:T(8,128)(2,1)S(1)}, bf16[1,512,512]{2,1,0:T(8,128)(2,1)}, u32[]{:S(2)}) copy-start(bf16[1,512,512]{2,1,0:T(8,128)(2,1)} %param.19) | copy-start | bytes 1572868
  7.2 1.5 %copy-start.6 = (f32[3,128]{1,0:T(4,128)S(1)}, f32[3,128]{1,0:T(4,128)}, u32[]{:S(2)}) copy-start(f32[3,128]{1,0:T(4,128)} %param.15) | copy-start | bytes 4612
  7.2 1.5 %copy-start.9 = (f32[128]{0:T(128)S(1)}, f32[128]{0:T(128)}, u32[]{:S(2)}) copy-start(f32[128]{0:T(128)} %param.14) | copy-start | bytes 1540
  7.2 1.5 %copy-start.7 = (f32[3,128]{1,0:T(4,128)S(1)}, f32[3,128]{1,0:T(4,128)}, u32[]{:S(2)}) copy-start(f32[3,128]{1,0:T(4,128)} %param.12) | copy-start | bytes 4612
  7.2 1.5 %copy-start.8 = (f32[2,128]{1,0:T(2,128)S(1)}, f32[2,128]{1,0:T(2,128)}, u32[]{:S(2)}) copy-start(f32[2,128]{1,0:T(2,128)} %param.13) | copy-start | bytes 3076
  7.2 8.0 %copy-start.4 = (bf16[96,128]{1,0:T(8,128)(2,1)S(1)}, bf16[96,128]{1,0:T(8,128)(2,1)}, u32[]{:S(2)}) copy-start(bf16[96,128]{1,0:T(8,128)(2,1)} %param.18) | copy-start | bytes 73732
  7.2 79.6 %reduce-scatter.7.cloned.1.call-start = ((), (), s32[]{:S(2)}) async-start(), calls=%async_computation.2 | async-start | bytes 163840
  8.6 17.7 %copy-start.3 = (s32[16,16]{1,0:T(8,128)S(1)}, s32[16,16]{1,0:T(8,128)}, u32[]{:S(2)}) copy-start(s32[16,16]{1,0:T(8,128)} %param.20) | copy-start | bytes 3076
  8.6 32.1 %copy-start.5 = (bf16[96,128]{1,0:T(8,128)(2,1)S(1)}, bf16[96,128]{1,0:T(8,128)(2,1)}, u32[]{:S(2)}) copy-start(bf16[96,128]{1,0:T(8,128)(2,1)} %param.17) | copy-start | bytes 73732
  15.1 37.7 %copy-start.1 = (s32[4]{0:T(128)S(1)}, s32[4]{0:T(128)}, u32[]{:S(2)}) copy-start(s32[4]{0:T(128)} %param.21) | copy-start | bytes 52
  66.4 21.3 %copy-start.2 = (f32[96,128]{1,0:T(8,128)S(1)}, f32[96,128]{1,0:T(8,128)}, u32[]{:S(2)}) copy-start(f32[96,128]{1,0:T(8,128)} %param.16) | copy-start | bytes 147460
  67.2 41.3 %reduce-scatter.9.cloned.1.call-start = ((), (), s32[]{:S(2)}) async-start(), calls=%async_computation.3 | async-start | bytes 163840
Sparse Core Ops, SparseCore 0:
  67.3 19.4 reduce-scatter.6
  89.0 19.4 reduce-scatter.8
where the time goes:
time: 117 us
  blocking collectives  48.3 us (41%)
  waiting for transfers between devices  33.3 us (28%)
  between operations  14.3 us (12%)
  local copies, waits for them, and re-layouts  9.36 us (8%)
  other arithmetic  8.2 us (7%)
  matrix products  2 us (2%)
  loops' own time  1.33 us (1%)
    unnamed x4, waiting for transfers between devices  33.3 us
    all_gather x1, blocking collectives, local(): src_geom = lax.all_gather(own_geom, 'rows', axis=1, tiled=True)  13.6 us
    all_gather x1, blocking collectives, local(): piece = lax.all_gather(radiosity, 'rows', axis=1, tiled=True)  12.1 us
    all_gather x1, blocking collectives, local(): lax.all_gather(jnp.concatenate([own_geom, reflect], axis=0), ('cols', 'ch...  6.24 us
    all_gather x1, blocking collectives, local(): recv_cot = lax.all_gather(cotangent, ('cols', 'chan'), axis=1, tiled=True)  5.57 us
    all_gather x1, blocking collectives, local(): weight = lax.all_gather(weight_own, ('cols', 'chan'), axis=1, tiled=True)  5.36 us
    all_gather x1, blocking collectives, local(): lax.all_gather(terms.astype(jnp.bfloat16), ('cols', 'chan'), axis=1, tile...  5.36 us
    select_n x2, other arithmetic, column_block(): visible_sub = jnp.take(visible_rows, src_block, axis=1).astype(jnp.float32)  5.1 us
  transfers between devices with their start and end apart: 2, of which 2 were waited for; matrix products, arithmetic and copies ran while one was open for 2% of the time, Pallas kernels for 0%

commit v1 on v0

v1 whole, which is shorter than its diff:
```python
import jax
import jax.numpy as jnp
from jax import lax
from jax.experimental import pallas as pl
from jax.experimental.pallas import tpu as pltpu
from jax.sharding import PartitionSpec as P

CLUSTER = 512
SUB = 128
SUBS = CLUSTER // SUB
COLORS = 3
LANES = 128
GEO = 32
Q_ROWS = 9
Z_ROWS = 8

AXES = ("scene", "rows", "cols", "chan")
VMEM = pl.BlockSpec(memory_space=pltpu.VMEM)
SMEM = pl.BlockSpec(memory_space=pltpu.SMEM)


def parity(bits):
    return bin(bits).count("1") % 2


def doubling_steps(size):
    if size & (size - 1):
        raise ValueError("axis size")
    return [2 << k | 1 for k in range(size.bit_length() - 1)]


def repeat(count, body):
    if count <= 4:
        for i in range(count):
            body(i)
    else:
        lax.fori_loop(0, count, lambda i, unused: (body(i), unused)[1], 0)


def swap(values, axes, size, mask):
    return lax.ppermute(values, axes, [(i, i ^ mask) for i in range(size)])


def row_block(index):
    col = lax.axis_index("cols") ^ (index >> 1)
    chan = lax.axis_index("chan") ^ ((index & 1) ^ parity(index >> 1))
    return col * 2 + chan


def three_parts(values):
    upper = values.astype(jnp.bfloat16)
    rest = values - upper.astype(jnp.float32)
    middle = rest.astype(jnp.bfloat16)
    lower = rest - middle.astype(jnp.float32)
    return upper.astype(jnp.float32), middle.astype(jnp.float32), lower


def pack_kernel(pos_ref, tilt_ref, area_ref, reflect_ref, rad_ref, cot_ref, z_ref, q_ref, geo):
    channels = rad_ref.shape[0]
    a = tilt_ref[0:1, :]
    b = tilt_ref[1:2, :]
    geo[...] = jnp.zeros_like(geo)
    geo[0:3, :] = pos_ref[...]
    geo[3:4, :] = jnp.cos(a) * jnp.cos(b)
    geo[4:5, :] = jnp.sin(a) * jnp.cos(b)
    geo[5:6, :] = jnp.sin(b)
    geo[6:7, :] = area_ref[...]
    parts = three_parts(geo[0:8, :])
    z_ref[0:channels, :] = rad_ref[...]
    packed = jnp.concatenate([*parts, jnp.zeros_like(parts[0])], axis=0)
    z_ref[channels:, :] = packed.astype(jnp.bfloat16)
    geo[6:9, :] = reflect_ref[...]
    parts = three_parts(geo[0:16, :])
    for k in range(3):
        geo[k * Q_ROWS : (k + 1) * Q_ROWS, :] = parts[k][0:Q_ROWS, :]
    q_ref[0:channels, :] = cot_ref[...]
    q_ref[channels:, :] = geo[...].astype(jnp.bfloat16)


def visible_kernel(blocks, subs, vis_ref, ids_ref, keep_ref):
    row = lax.axis_index("rows")
    col = lax.axis_index("cols")
    chan = lax.axis_index("chan")
    first = row * (subs * SUB // CLUSTER)
    for b in range(blocks):
        slot = (row ^ b) * subs + col * 2 + (chan ^ parity(b))
        src_cluster = slot // SUBS
        src_block = ids_ref[src_cluster] * SUBS + lax.rem(slot, SUBS)
        for t in range(subs):
            recv_cluster = first + t // SUBS
            seen = vis_ref[ids_ref[recv_cluster] * SUBS + t % SUBS, src_block]
            seen = jnp.where(recv_cluster != src_cluster, seen, 0)
            keep_ref[b * subs + t : b * subs + t + 1, :] = jnp.full((1, LANES), seen.astype(jnp.float32))


def spread_rows(rows, targets):
    part = lax.broadcasted_iota(jnp.int32, (GEO, targets), 0)
    hit = (part == rows) | (part == rows + Q_ROWS) | (part == rows + 2 * Q_ROWS)
    return hit.astype(jnp.float32).astype(jnp.bfloat16)


def factor_tile(block_ref, start, channels, keep_ref, keep_row, geo_ref, tile_ref, lane):
    parts = block_ref[pl.ds(start + channels, GEO), :].astype(jnp.float32)
    src = parts[0:8, :] + parts[8:16, :] + parts[16:24, :]
    area = src[6:7, :]

    def receivers(t):
        at = pl.ds(t * SUB, SUB)
        v = [src[k : k + 1, :] - geo_ref[k, at, :] for k in range(3)]
        distance = v[0] * v[0] + v[1] * v[1] + v[2] * v[2]
        facing = geo_ref[3, at, :] * v[0] + geo_ref[4, at, :] * v[1] + geo_ref[5, at, :] * v[2]
        behind = -(src[3:4, :] * v[0] + src[4:5, :] * v[1] + src[5:6, :] * v[2])
        spread = distance + area
        scale = area * keep_ref[pl.ds(keep_row + t, 1), :]
        value = jnp.maximum(facing, 0.0) * jnp.maximum(behind, 0.0) * scale / (jnp.pi * spread * spread)
        tile_ref[at, pl.ds(lane * SUB, SUB)] = value.astype(jnp.bfloat16)

    repeat(tile_ref.shape[0] // SUB, receivers)


ROW_BY_ROW = (((1,), (1,)), ((), ()))


def dot(a, b, dims=(((1,), (0,)), ((), ()))):
    return lax.dot_general(a, b, dims, preferred_element_type=jnp.float32)


def sources(blocks, first, block_ref, keep_ref, geo_ref, weight_ref, tile_ref):
    channels, receivers = weight_ref.shape
    height = channels + GEO
    subs = receivers // SUB
    repeat(
        blocks,
        lambda i: factor_tile(block_ref, i * height, channels, keep_ref, (first + i) * subs, geo_ref, tile_ref, i),
    )
    tile = tile_ref[...]
    rad = jnp.concatenate([block_ref[i * height : i * height + channels, :] for i in range(blocks)], axis=1)
    return dot(rad, tile, ROW_BY_ROW), dot(weight_ref[...], tile)


def early_kernel(
    near_ref, far_ref, src_ref, keep_ref, inv_ref, weight_ref, geo_ref, rho_ref, fwd_ref, grad_ref, cot_ref, tile_ref
):
    channels, receivers = weight_ref.shape
    height = channels + GEO
    half = near_ref.shape[0] // height
    color = lax.rem(lax.broadcasted_iota(jnp.int32, (GEO, channels), 1), COLORS)
    pick_rho = spread_rows(6 + color, channels)
    for b in range(2 * half):
        ref, at = (near_ref, b) if b < half else (far_ref, b - half)
        lanes = pl.ds(pl.multiple_of(row_block(b) * SUB, SUB), SUB)
        cot_ref[:, lanes] = ref[at * height : at * height + channels, :]
        parts = ref[at * height + channels : (at + 1) * height, :]
        rho_ref[:, lanes] = dot(pick_rho, parts, (((0,), (0,)), ((), ())))
        for k in range(6):
            geo_ref[k, lanes, :] = dot(parts, spread_rows(k, LANES), (((0,), (0,)), ((), ())))
    for k in range(receivers // CLUSTER):
        at = slice(k * CLUSTER, (k + 1) * CLUSTER)
        weight_ref[:, at] = (rho_ref[:, at] * dot(cot_ref[:, at], inv_ref[k])).astype(jnp.bfloat16)
    blocks = grad_ref.shape[0] // channels
    fwd, grad = sources(blocks, 0, src_ref, keep_ref, geo_ref, weight_ref, tile_ref)
    fwd_ref[...] = fwd
    for i in range(blocks):
        grad_ref[i * channels : (i + 1) * channels, :] = grad[:, i * SUB : (i + 1) * SUB]


def late_kernel(
    src_ref,
    keep_ref,
    inv_ref,
    weight_ref,
    geo_ref,
    rho_ref,
    fwd_ref,
    emission_ref,
    grad_ref,
    near_ref,
    far_ref,
    terms_ref,
    solved_ref,
    tile_ref,
):
    channels, receivers = weight_ref.shape
    blocks = grad_ref.shape[0] // channels
    fwd, grad = sources(blocks, blocks, src_ref, keep_ref, geo_ref, weight_ref, tile_ref)
    for i in range(blocks):
        grad_ref[i * channels : (i + 1) * channels, :] = grad[:, i * SUB : (i + 1) * SUB].astype(jnp.bfloat16)
    terms_ref[...] = rho_ref[...] * (fwd_ref[...] + fwd)
    own = pl.ds(pl.multiple_of(row_block(0) * SUB, SUB), SUB)
    terms_ref[:, own] = terms_ref[:, own] + emission_ref[...]
    for k in range(receivers // CLUSTER):
        at = slice(k * CLUSTER, (k + 1) * CLUSTER)
        terms = terms_ref[:, at]
        upper = terms.astype(jnp.bfloat16)
        lower = (terms - upper.astype(jnp.float32)).astype(jnp.bfloat16)
        solved_ref[:, at] = dot(upper, inv_ref[k], ROW_BY_ROW) + dot(lower, inv_ref[k], ROW_BY_ROW)
    half = near_ref.shape[0] // channels
    for b in range(2 * half):
        lanes = pl.ds(pl.multiple_of(row_block(b) * SUB, SUB), SUB)
        if b < half:
            near_ref[b * channels : (b + 1) * channels, :] = solved_ref[:, lanes]
        else:
            far_ref[(b - half) * channels : (b - half + 1) * channels, :] = solved_ref[:, lanes].astype(jnp.bfloat16)


def halving(kept, sent, axes, size, masks):
    while True:
        kept = kept + swap(sent, axes, size, masks[-1]).astype(jnp.float32)
        masks = masks[:-1]
        if not masks:
            return kept
        half = kept.shape[0] // 2
        kept, sent = kept[:half], kept[half:].astype(jnp.bfloat16)


def local(
    position, tilt, patch_area, reflect, emission, radiosity, cotangent, block_inverse, visibility, cluster_ids
):
    channels, dev_patches = radiosity.shape
    rows, cols, chan = (lax.axis_size(name) for name in ("rows", "cols", "chan"))
    if dev_patches != SUB or chan != 2 or rows < 2 or cols < 2:
        raise ValueError("split")
    subs = cols * chan
    receivers = subs * SUB
    height = channels + GEO
    f32, bf16 = jnp.float32, jnp.bfloat16
    q_axes, q_masks = ("cols", "chan"), [1, *doubling_steps(cols)]
    z_axes, z_masks = ("rows", "chan"), doubling_steps(rows)

    z_block, q_block = pl.pallas_call(
        pack_kernel,
        out_shape=[jax.ShapeDtypeStruct((height, SUB), bf16)] * 2,
        in_specs=[VMEM] * 6,
        out_specs=[VMEM] * 2,
        scratch_shapes=[pltpu.VMEM((GEO, SUB), f32)],
        name="pack",
    )(position, tilt, patch_area[None, :], reflect, radiosity, cotangent)

    keep = pl.pallas_call(
        lambda *refs: visible_kernel(rows, subs, *refs),
        out_shape=jax.ShapeDtypeStruct((rows * subs, LANES), f32),
        in_specs=[SMEM] * 2,
        out_specs=VMEM,
        name="visible",
    )(visibility, cluster_ids)

    q_near, z_near = q_block, z_block
    for mask in q_masks[:-1]:
        q_near = jnp.concatenate([q_near, swap(q_near, q_axes, subs, mask)], axis=0)
    for mask in z_masks[:-1]:
        z_near = jnp.concatenate([z_near, swap(z_near, z_axes, rows * chan, mask)], axis=0)
    q_far = swap(q_near, q_axes, subs, q_masks[-1])
    z_far = swap(z_near, z_axes, rows * chan, z_masks[-1])

    blocks = rows // 2
    weight, geo, rho, fwd, grad_near = pl.pallas_call(
        early_kernel,
        out_shape=[
            jax.ShapeDtypeStruct((channels, receivers), bf16),
            jax.ShapeDtypeStruct((6, receivers, LANES), f32),
            jax.ShapeDtypeStruct((channels, receivers), f32),
            jax.ShapeDtypeStruct((channels, receivers), f32),
            jax.ShapeDtypeStruct((blocks * channels, SUB), f32),
        ],
        in_specs=[VMEM] * 5,
        out_specs=[VMEM] * 5,
        scratch_shapes=[pltpu.VMEM((channels, receivers), bf16), pltpu.VMEM((receivers, blocks * SUB), bf16)],
        name="early",
    )(q_near, q_far, z_near, keep, block_inverse)

    grad_far, solved_near, solved_far = pl.pallas_call(
        late_kernel,
        out_shape=[
            jax.ShapeDtypeStruct((blocks * channels, SUB), bf16),
            jax.ShapeDtypeStruct((subs // 2 * channels, SUB), f32),
            jax.ShapeDtypeStruct((subs // 2 * channels, SUB), bf16),
        ],
        in_specs=[VMEM] * 8,
        out_specs=[VMEM] * 3,
        scratch_shapes=[
            pltpu.VMEM((channels, receivers), f32),
            pltpu.VMEM((channels, receivers), f32),
            pltpu.VMEM((receivers, blocks * SUB), bf16),
        ],
        name="late",
    )(z_far, keep, block_inverse, weight, geo, rho, fwd, emission)

    gradient = halving(grad_near, grad_far, z_axes, rows * chan, z_masks)
    solved = halving(solved_near, solved_far, q_axes, subs, q_masks)
    return solved.astype(bf16), gradient


def solution(mesh):
    split = P(None, AXES)
    return jax.shard_map(
        local,
        mesh=mesh,
        in_specs=(
            split,
            split,
            P(AXES),
            split,
            split,
            split,
            split,
            P(("scene", "rows"), None, None),
            P("scene", None),
            P("scene"),
        ),
        out_specs=(split, split),
        check_vma=False,
    )
```

time: 117 us -> 29.8 us (0.25)
  blocking collectives: 48.3 us -> 0 us
  waiting for transfers between devices: 33.3 us -> 2.69 us
  between operations: 14.3 us -> 0.69 us
  starting transfers between devices: 0.08 us -> 11.4 us
  Pallas kernels: 0 us -> 9.6 us
  local copies, waits for them, and re-layouts: 9.36 us -> 2.79 us
  other arithmetic: 8.2 us -> 2.17 us
  matrix products: 2 us -> 0 us
  loops' own time: 1.33 us -> 0 us
    all_gather x6 -> x0, blocking collectives: 48.3 us -> none  [the longest x1 13.6 us: local(): src_geom = lax.all_gather(own_geom, 'rows', axis=1, tiled=True)]
    unnamed x4 -> x0, waiting for transfers between devices: 33.3 us -> none
    ppermute x0 -> x8, starting transfers between devices: none -> 11.4 us  [swap(): return lax.ppermute(values, axes, [(i, i ^ mask) for i in range(size)])]
    pallas_call x0 -> x4, Pallas kernels: none -> 9.6 us  [the longest x1 3.58 us: local(): pl.pallas_call(late_kernel, out_shape=[jax.ShapeDtypeStruct((blocks * cha...]
    select_n x9 -> x0, other arithmetic: 5.27 us -> none  [the longest x2 5.1 us: column_block(): visible_sub = jnp.take(visible_rows, src_block, axis=1).astype(jnp.float32)]
    gather x6 -> x0, local copies, waits for them, and re-layouts: 4.62 us -> none  [the longest x2 1.46 us: column_block(): visible_sub = jnp.take(visible_rows, src_block, axis=1).astype(jnp.float32)]
    ppermute x0 -> x8, waiting for transfers between devices: none -> 2.69 us  [swap(): return lax.ppermute(values, axes, [(i, i ^ mask) for i in range(size)])]
    dot_general x7 -> x0, matrix products: 2 us -> none  [the longest x1 0.81 us: local(): lax.dot_general(lower, inverse_rows, dims, preferred_element_type=jnp.flo...]
  transfers between devices with their start and end apart: 2 -> 8, of which waited for: 2 -> 3; matrix products, arithmetic and copies ran while one was open for 2% -> 11% of each run, Pallas kernels for 0% -> 15%
where the time goes in v1:
time: 29.8 us; the launch traced here: 29.4 us
  starting transfers between devices  11.4 us (38%)
  Pallas kernels  9.6 us (32%)
  local copies, waits for them, and re-layouts  2.79 us (9%)
  waiting for transfers between devices  2.69 us (9%)
  other arithmetic  2.17 us (7%)
  between operations  0.69 us (2%)
    ppermute x8, starting transfers between devices, swap(): return lax.ppermute(values, axes, [(i, i ^ mask) for i in range(size)])  11.4 us
    pallas_call x1, Pallas kernels, local(): pl.pallas_call(late_kernel, out_shape=[jax.ShapeDtypeStruct((blocks * cha...  3.58 us
    pallas_call x1, Pallas kernels, local(): pl.pallas_call(early_kernel, out_shape=[jax.ShapeDtypeStruct((channels, r...  3.04 us
    unnamed x12, local copies, waits for them, and re-layouts  2.76 us
    ppermute x8, waiting for transfers between devices, swap(): return lax.ppermute(values, axes, [(i, i ^ mask) for i in range(size)])  2.69 us
    add x3, other arithmetic, halving(): kept = kept + swap(sent, axes, size, masks[-1]).astype(jnp.float32)  1.55 us
    pallas_call x1, Pallas kernels, local(): pl.pallas_call(pack_kernel, out_shape=[jax.ShapeDtypeStruct((height, SUB)...  1.5 us
    pallas_call x1, Pallas kernels, local(): pl.pallas_call(lambda *refs: visible_kernel(rows, subs, *refs), out_shape...  1.48 us
  transfers between devices with their start and end apart: 8, of which 3 were waited for; matrix products, arithmetic and copies ran while one was open for 11% of the time, Pallas kernels for 15%

profile of v1, /device:TPU:0, one launch (start us, length us, event | category | flops | bytes accessed | tf_op | source)
XLA Modules:
  0.0 29.4 jit_solution(17231822031592838950)
XLA Ops:
  0.6 1.5 %pack.1 = (bf16[128,128]{1,0:T(8,128)(2,1)}, bf16[128,128]{1,0:T(8,128)(2,1)}) custom-call(f32[3,128]{1,0:T(4,128)} %pos_ref.1, f32[2,128]{1,0:T(2,128)} %tilt_ref.1, f32[1,128]{1,0:T(1,128)} %bitcast.1, f32[3,128]{1,0:T(4,128)} %reflect_ref.1, bf16[96,128]{1,0:T(8,128)(2,1)} %rad_ref.1, bf16[96,128]{1,0:T(8,128)(2,1)} %cot_ref.1), custom_call_target="tpu_custom_call" | custom-call | tf_op jit(solution)/shard_map/pack/pallas_call | solution.py:230
  2.1 2.5 %collective-permute-start = (bf16[128,128]{1,0:T(8,128)(2,1)}, bf16[128,128]{1,0:T(8,128)(2,1)S(1)}, u32[]{:S(2)}, u32[]{:S(2)}) collective-permute-start(bf16[128,128]{1,0:T(8,128)(2,1)} %get-tuple-element.12), channel_id=1, source_target_pairs={{0,5},{1,4},{4,1},{5,0},{8,13},{9,12},{12,9},{13,8},{2,7},{3,6},{6... | collective-permute-start | bytes 98312 | tf_op jit(solution)/shard_map/ppermute | solution.py:41
  4.6 0.7 %collective-permute-start.2 = (bf16[128,128]{1,0:T(8,128)(2,1)}, bf16[128,128]{1,0:T(8,128)(2,1)S(1)}, u32[]{:S(2)}, u32[]{:S(2)}) collective-permute-start(bf16[128,128]{1,0:T(8,128)(2,1)} %get-tuple-element.13), channel_id=1, source_target_pairs={{0,1},{1,0},{2,3},{3,2},{4,5},{5,4},{6,7},{7,6},{8,9},{9,8},{10,11... | collective-permute-start | bytes 98312 | tf_op jit(solution)/shard_map/ppermute | solution.py:41
  5.3 0.8 %constant_dynamic-update-slice_fusion.1 = bf16[256,128]{1,0:T(8,128)(2,1)S(1)} fusion(bf16[128,128]{1,0:T(8,128)(2,1)} %get-tuple-element.12), kind=kLoop, calls=%fused_computation.8 | loop fusion | bytes 65536
  6.1 0.8 %constant_dynamic-update-slice_fusion.3 = bf16[256,128]{1,0:T(8,128)(2,1)S(1)} fusion(bf16[128,128]{1,0:T(8,128)(2,1)} %get-tuple-element.13), kind=kLoop, calls=%fused_computation.10 | loop fusion | bytes 65536
  6.8 0.0 collective-permute-done.2
  6.8 0.0 copy-start.1
  6.8 1.2 %collective-permute-start.3 = (bf16[256,128]{1,0:T(8,128)(2,1)S(1)}, bf16[256,128]{1,0:T(8,128)(2,1)S(1)}, u32[]{:S(2)}, u32[]{:S(2)}) collective-permute-start(bf16[256,128]{1,0:T(8,128)(2,1)S(1)} %constant_dynamic-update-slice_fusion.2.near_ref), channel_id=1, source_target_pairs={{0,3},{1,2},{2,1},{3,0},{4,7},{5,6},{6,5},{7,4},{8,11},{9,10},{10,... | collective-permute-start | bytes 196616 | tf_op jit(solution)/shard_map/ppermute | solution.py:41
  8.0 0.0 collective-permute-done
  8.1 0.0 copy-start
  8.1 2.7 %collective-permute-start.1 = (bf16[256,128]{1,0:T(8,128)(2,1)S(1)}, bf16[256,128]{1,0:T(8,128)(2,1)S(1)}, u32[]{:S(2)}, u32[]{:S(2)}) collective-permute-start(bf16[256,128]{1,0:T(8,128)(2,1)S(1)} %constant_dynamic-update-slice_fusion.src_ref), channel_id=1, source_target_pairs={{0,9},{1,8},{4,13},{5,12},{8,1},{9,0},{12,5},{13,4},{2,11},{3,10},... | collective-permute-start | bytes 196616 | tf_op jit(solution)/shard_map/ppermute | solution.py:41
  10.8 1.5 %visible.1.keep_ref = f32[16,128]{1,0:T(8,128)} custom-call(s32[16,16]{1,0:T(8,128)} %refs_0_.1, s32[4]{0:T(128)} %refs_1_.1), custom_call_target="tpu_custom_call" | custom-call | tf_op jit(solution)/shard_map/visible/pallas_call | solution.py:239
  12.3 0.0 collective-permute-done.3.far_ref
  12.3 0.0 copy-done.1
  12.3 0.0 copy-done
  12.3 0.0 copy-start.3
  12.3 0.6 %copy-done.3 = bf16[256,128]{1,0:T(8,128)(2,1)} copy-done((bf16[256,128]{1,0:T(8,128)(2,1)}, bf16[256,128]{1,0:T(8,128)(2,1)S(1)}, u32[]{:S(2)}) %copy-start.3) | copy-done | bytes 65560
  12.9 3.0 %early.1 = (bf16[96,512]{1,0:T(8,128)(2,1)}, f32[6,512,128]{2,1,0:T(8,128)}, f32[96,512]{1,0:T(8,128)}, f32[96,512]{1,0:T(8,128)}, f32[192,128]{1,0:T(8,128)}) custom-call(bf16[256,128]{1,0:T(8,128)(2,1)} %copy-done.1, bf16[256,128]{1,0:T(8,128)(2,1)} %copy-done.3, bf16[256,128]{1,0:T(8,128)(2,1)} %copy-done, f32[16,128]{1,0:T(8,128)} %visible.1.keep_ref, ...), custom_call_target="tpu_custom_call" | custom-call | tf_op jit(solution)/shard_map/early/pallas_call | solution.py:256
  15.9 0.0 copy-start.2
  15.9 0.0 collective-permute-done.1.src_ref
  15.9 0.0 copy-start.4
  16.0 0.6 %copy-done.4 = bf16[256,128]{1,0:T(8,128)(2,1)} copy-done((bf16[256,128]{1,0:T(8,128)(2,1)}, bf16[256,128]{1,0:T(8,128)(2,1)S(1)}, u32[]{:S(2)}) %copy-start.4) | copy-done | bytes 65560
  16.6 3.6 %late.1 = (bf16[192,128]{1,0:T(8,128)(2,1)}, f32[192,128]{1,0:T(8,128)}, bf16[192,128]{1,0:T(8,128)(2,1)}) custom-call(bf16[256,128]{1,0:T(8,128)(2,1)} %copy-done.4, f32[16,128]{1,0:T(8,128)} %visible.1.keep_ref, bf16[1,512,512]{2,1,0:T(8,128)(2,1)} %inv_ref.3, bf16[96,512]{1,0:T(8,128)(2,1)} %get-tuple-element.14.weight_ref, ...), custom_call_target="tpu_custom_call" | custom-call | tf_op jit(solution)/shard_map/late/pallas_call | solution.py:271
  20.2 0.5 %collective-permute-start.4 = (bf16[192,128]{1,0:T(8,128)(2,1)}, bf16[192,128]{1,0:T(8,128)(2,1)S(1)}, u32[]{:S(2)}, u32[]{:S(2)}) collective-permute-start(bf16[192,128]{1,0:T(8,128)(2,1)} %get-tuple-element.19), channel_id=1, source_target_pairs={{0,3},{1,2},{2,1},{3,0},{4,7},{5,6},{6,5},{7,4},{8,11},{9,10},{10,... | collective-permute-start | bytes 147464 | tf_op jit(solution)/shard_map/ppermute | solution.py:41
  20.6 2.1 %collective-permute-start.6 = (bf16[192,128]{1,0:T(8,128)(2,1)}, bf16[192,128]{1,0:T(8,128)(2,1)S(1)}, u32[]{:S(2)}, u32[]{:S(2)}) collective-permute-start(bf16[192,128]{1,0:T(8,128)(2,1)} %get-tuple-element.21), channel_id=1, source_target_pairs={{0,9},{1,8},{4,13},{5,12},{8,1},{9,0},{12,5},{13,4},{2,11},{3,10},... | collective-permute-start | bytes 147464 | tf_op jit(solution)/shard_map/ppermute | solution.py:41
  22.8 1.4 %collective-permute-done.4 = bf16[192,128]{1,0:T(8,128)(2,1)S(1)} collective-permute-done((bf16[192,128]{1,0:T(8,128)(2,1)}, bf16[192,128]{1,0:T(8,128)(2,1)S(1)}, u32[]{:S(2)}, u32[]{:S(2)}) %collective-permute-start.4) | collective-permute-done | bytes 49184 | tf_op jit(solution)/shard_map/ppermute | solution.py:41
  24.2 0.9 %convert_add_fusion.1 = f32[192,128]{1,0:T(8,128)S(1)} fusion(f32[192,128]{1,0:T(8,128)} %get-tuple-element.18, bf16[192,128]{1,0:T(8,128)(2,1)S(1)} %collective-permute-done.4), kind=kLoop, calls=%fused_computation.1 | loop fusion | flops 49152 | bytes 245760 | tf_op jit(solution)/shard_map/add | solution.py:208
  25.1 0.2 collective-permute-start.5
  25.3 0.1 collective-permute-done.6
  25.4 0.0 copy-done.2
  25.4 1.6 %collective-permute-start.7 = (bf16[96,128]{1,0:T(8,128)(2,1)S(1)}, bf16[96,128]{1,0:T(8,128)(2,1)S(1)}, u32[]{:S(2)}, u32[]{:S(2)}) collective-permute-start(bf16[96,128]{1,0:T(8,128)(2,1)S(1)} %slice.28), channel_id=1, source_target_pairs={{0,5},{1,4},{4,1},{5,0},{8,13},{9,12},{12,9},{13,8},{2,7},{3,6},{6... | collective-permute-start | bytes 73736 | tf_op jit(solution)/shard_map/ppermute | solution.py:41
  27.0 0.0 collective-permute-done.5
  27.0 0.6 %fusion = bf16[96,128]{1,0:T(8,128)(2,1)} fusion(f32[192,128]{1,0:T(8,128)S(1)} %convert_add_fusion.1, bf16[96,128]{1,0:T(8,128)(2,1)S(1)} %collective-permute-done.5), kind=kLoop, calls=%fused_computation.6 | loop fusion | flops 36864 | bytes 98304 | tf_op jit(solution)/shard_map/convert_element_type | solution.py:290
  27.6 1.1 %collective-permute-done.7 = bf16[96,128]{1,0:T(8,128)(2,1)S(1)} collective-permute-done((bf16[96,128]{1,0:T(8,128)(2,1)S(1)}, bf16[96,128]{1,0:T(8,128)(2,1)S(1)}, u32[]{:S(2)}, u32[]{:S(2)}) %collective-permute-start.7) | collective-permute-done | bytes 24608 | tf_op jit(solution)/shard_map/ppermute | solution.py:41
  28.8 0.6 %slice_add_fusion = f32[96,128]{1,0:T(8,128)} fusion(f32[192,128]{1,0:T(8,128)S(1)} %convert_add_fusion, bf16[96,128]{1,0:T(8,128)(2,1)S(1)} %collective-permute-done.7), kind=kLoop, calls=%fused_computation.3 | loop fusion | flops 24576 | bytes 122880 | tf_op jit(solution)/shard_map/add | solution.py:208
  (5 shorter events, 0.0 us)
Async XLA Ops:
  2.1 5.9 %collective-permute-start = (bf16[128,128]{1,0:T(8,128)(2,1)}, bf16[128,128]{1,0:T(8,128)(2,1)S(1)}, u32[]{:S(2)}, u32[]{:S(2)}) collective-permute-start(bf16[128,128]{1,0:T(8,128)(2,1)} %get-tuple-element.12), channel_id=1, source_target_pairs={{0,5},{1,4},{4,1},{5,0},{8,13},{9,12},{12,9},{13,8},{2,7},{3,6},{6... | collective-permute-start | bytes 98312 | tf_op jit(solution)/shard_map/ppermute | solution.py:41
  4.6 2.2 %collective-permute-start.2 = (bf16[128,128]{1,0:T(8,128)(2,1)}, bf16[128,128]{1,0:T(8,128)(2,1)S(1)}, u32[]{:S(2)}, u32[]{:S(2)}) collective-permute-start(bf16[128,128]{1,0:T(8,128)(2,1)} %get-tuple-element.13), channel_id=1, source_target_pairs={{0,1},{1,0},{2,3},{3,2},{4,5},{5,4},{6,7},{7,6},{8,9},{9,8},{10,11... | collective-permute-start | bytes 98312 | tf_op jit(solution)/shard_map/ppermute | solution.py:41
  6.8 5.4 %copy-start.1 = (bf16[256,128]{1,0:T(8,128)(2,1)}, bf16[256,128]{1,0:T(8,128)(2,1)S(1)}, u32[]{:S(2)}) copy-start(bf16[256,128]{1,0:T(8,128)(2,1)S(1)} %constant_dynamic-update-slice_fusion.2.near_ref) | copy-start | bytes 196612
  6.8 5.4 %collective-permute-start.3 = (bf16[256,128]{1,0:T(8,128)(2,1)S(1)}, bf16[256,128]{1,0:T(8,128)(2,1)S(1)}, u32[]{:S(2)}, u32[]{:S(2)}) collective-permute-start(bf16[256,128]{1,0:T(8,128)(2,1)S(1)} %constant_dynamic-update-slice_fusion.2.near_ref), channel_id=1, source_target_pairs={{0,3},{1,2},{2,1},{3,0},{4,7},{5,6},{6,5},{7,4},{8,11},{9,10},{10,... | collective-permute-start | bytes 196616 | tf_op jit(solution)/shard_map/ppermute | solution.py:41
  8.1 4.2 %copy-start = (bf16[256,128]{1,0:T(8,128)(2,1)}, bf16[256,128]{1,0:T(8,128)(2,1)S(1)}, u32[]{:S(2)}) copy-start(bf16[256,128]{1,0:T(8,128)(2,1)S(1)} %constant_dynamic-update-slice_fusion.src_ref) | copy-start | bytes 196612
  8.1 7.9 %collective-permute-start.1 = (bf16[256,128]{1,0:T(8,128)(2,1)S(1)}, bf16[256,128]{1,0:T(8,128)(2,1)S(1)}, u32[]{:S(2)}, u32[]{:S(2)}) collective-permute-start(bf16[256,128]{1,0:T(8,128)(2,1)S(1)} %constant_dynamic-update-slice_fusion.src_ref), channel_id=1, source_target_pairs={{0,9},{1,8},{4,13},{5,12},{8,1},{9,0},{12,5},{13,4},{2,11},{3,10},... | collective-permute-start | bytes 196616 | tf_op jit(solution)/shard_map/ppermute | solution.py:41
  12.3 0.6 %copy-start.3 = (bf16[256,128]{1,0:T(8,128)(2,1)}, bf16[256,128]{1,0:T(8,128)(2,1)S(1)}, u32[]{:S(2)}) copy-start(bf16[256,128]{1,0:T(8,128)(2,1)S(1)} %collective-permute-done.3.far_ref) | copy-start | bytes 196612
  15.9 9.5 %copy-start.2 = (f32[192,128]{1,0:T(8,128)S(1)}, f32[192,128]{1,0:T(8,128)}, u32[]{:S(2)}) copy-start(f32[192,128]{1,0:T(8,128)} %get-tuple-element.20) | copy-start | bytes 294916
  15.9 0.6 %copy-start.4 = (bf16[256,128]{1,0:T(8,128)(2,1)}, bf16[256,128]{1,0:T(8,128)(2,1)S(1)}, u32[]{:S(2)}) copy-start(bf16[256,128]{1,0:T(8,128)(2,1)S(1)} %collective-permute-done.1.src_ref) | copy-start | bytes 196612
  20.2 4.0 %collective-permute-start.4 = (bf16[192,128]{1,0:T(8,128)(2,1)}, bf16[192,128]{1,0:T(8,128)(2,1)S(1)}, u32[]{:S(2)}, u32[]{:S(2)}) collective-permute-start(bf16[192,128]{1,0:T(8,128)(2,1)} %get-tuple-element.19), channel_id=1, source_target_pairs={{0,3},{1,2},{2,1},{3,0},{4,7},{5,6},{6,5},{7,4},{8,11},{9,10},{10,... | collective-permute-start | bytes 147464 | tf_op jit(solution)/shard_map/ppermute | solution.py:41
  20.6 4.8 %collective-permute-start.6 = (bf16[192,128]{1,0:T(8,128)(2,1)}, bf16[192,128]{1,0:T(8,128)(2,1)S(1)}, u32[]{:S(2)}, u32[]{:S(2)}) collective-permute-start(bf16[192,128]{1,0:T(8,128)(2,1)} %get-tuple-element.21), channel_id=1, source_target_pairs={{0,9},{1,8},{4,13},{5,12},{8,1},{9,0},{12,5},{13,4},{2,11},{3,10},... | collective-permute-start | bytes 147464 | tf_op jit(solution)/shard_map/ppermute | solution.py:41
  25.1 1.9 %collective-permute-start.5 = (bf16[96,128]{1,0:T(8,128)(2,1)S(1)}, bf16[96,128]{1,0:T(8,128)(2,1)S(1)}, u32[]{:S(2)}, u32[]{:S(2)}) collective-permute-start(bf16[96,128]{1,0:T(8,128)(2,1)S(1)} %slice.29), channel_id=1, source_target_pairs={{0,1},{1,0},{2,3},{3,2},{4,5},{5,4},{6,7},{7,6},{8,9},{9,8},{10,11... | collective-permute-start | bytes 73736 | tf_op jit(solution)/shard_map/ppermute | solution.py:41
  25.4 3.3 %collective-permute-start.7 = (bf16[96,128]{1,0:T(8,128)(2,1)S(1)}, bf16[96,128]{1,0:T(8,128)(2,1)S(1)}, u32[]{:S(2)}, u32[]{:S(2)}) collective-permute-start(bf16[96,128]{1,0:T(8,128)(2,1)S(1)} %slice.28), channel_id=1, source_target_pairs={{0,5},{1,4},{4,1},{5,0},{8,13},{9,12},{12,9},{13,8},{2,7},{3,6},{6... | collective-permute-start | bytes 73736 | tf_op jit(solution)/shard_map/ppermute | solution.py:41
